TPU v7x, 512 devices: a whole 4x4x16 slice. The times are simulated.
512 devices in a mesh: tok: 8 (over x, core), dict: 64 (over z, y).
Axes of the slice: x: 4, y: 4, z: 16, core: 2. Of those that a mesh axis runs over, the one named last changes fastest.
Arguments:
- inputs: bfloat16 [4096, 4608], P('tok', 'dict'), may hold values from -6 to 6
- target: bfloat16 [4096, 4608], P('tok', 'dict'), may hold values from -6 to 6
- enc_weight: bfloat16 [4608, 8192], P(None, 'dict'), may hold values from -0.09375 to 0.09375
- enc_bias: float32 [8192], P('dict'), may hold values from -3 to 3
- dec_weight: bfloat16 [8192, 4608], P('dict'), may hold values from -0.75 to 0.75
- dec_bias: float32 [4608], P('dict'), may hold values from -3 to 3
- skip_weight: bfloat16 [4608, 4608], P(None, 'dict'), may hold values from -0.09375 to 0.09375
- block_ids: int32 [4096, 4], P('tok'), may hold values from 0 to 511, as said below
- slot_lists: int32 [8, 64, 96], P('tok'), may hold values from 0 to 2047, as said below
- slot_counts: int32 [8, 64], P('tok'), may hold values from 0 to 96, as said below
Outputs:
- grad_enc: float32 [4608, 8192], P('tok', 'dict')
- grad_dec: float32 [8192, 4608], P('dict', 'tok')
- grad_skip: float32 [4608, 4608], P('tok', 'dict')
Inputs may be any that keep to these rules, and one draw needn't show every extreme that they name: `block_ids`: each token names 4 different blocks of 16 latents. `slot_lists`: A valid slot of list (g, o) holds a code index t * 4 + r of group g (its token t, the token's r-th block); every code of a group stands in exactly one valid slot, in the list of the owner of its block; invalid slots hold 0. `slot_counts`: in every group some list is full.
All inputs are finite; a program needn't handle non-finite values.
Results may differ from a plain program's by a relative error of at most 0.012.
Values may be sent and summed in bfloat16 or wider, within the bound.
No kernel may reach another device: no remote copies, remote signals or barrier semaphores. Data moves between devices by JAX's collectives and lax.ppermute only.
A program may use at most 64 MiB of HBM per device.

v0:
```python
import math

import jax
import jax.numpy as jnp
from jax import lax
from jax.sharding import PartitionSpec as P

BLK = 16


def gelu_pair(pre):
    factor = math.sqrt(2.0 / math.pi)
    inner = jnp.tanh(factor * (pre + 0.044715 * pre * pre * pre))
    value = 0.5 * pre * (1.0 + inner)
    slope = 0.5 * (1.0 + inner) + 0.5 * pre * (1.0 - inner * inner) * factor * (
        1.0 + 3.0 * 0.044715 * pre * pre
    )
    return (value, slope)


def local(
    inputs,
    target,
    enc_weight,
    enc_bias,
    dec_weight,
    dec_bias,
    skip_weight,
    block_ids,
    slot_lists,
    slot_counts,
):
    tok_rows, feat_dev = inputs.shape
    lat_dev = enc_weight.shape[1]
    capacity = slot_lists.shape[2]
    per_token = block_ids.shape[1]
    owner = lax.axis_index("dict")
    total_tokens = tok_rows * lax.axis_size("tok")
    scale = 1.0 / math.sqrt(total_tokens)
    whole = lax.all_gather(inputs, "dict", axis=1, tiled=True)
    slots_all = slot_lists[0]
    counts_all = slot_counts[0]
    valid_all = jnp.arange(capacity, dtype=jnp.int32)[None, :] < counts_all[:, None]
    rows_all = (slots_all // per_token).reshape(-1)
    my_slots = lax.dynamic_index_in_dim(slots_all, owner, 0, keepdims=False)
    my_valid = lax.dynamic_index_in_dim(valid_all, owner, 0, keepdims=False)
    my_rows = my_slots // per_token
    my_blocks = block_ids.reshape(-1)[my_slots]
    latent = owner * lat_dev + jnp.arange(lat_dev, dtype=jnp.int32)
    active = (latent[None, :] // BLK == my_blocks[:, None]) & my_valid[:, None]
    picked = whole[my_rows]
    pre = jnp.dot(picked, enc_weight, preferred_element_type=jnp.float32) + enc_bias[None, :]
    value, slope = gelu_pair(pre)
    code = jnp.where(active, value, 0.0).astype(jnp.bfloat16)
    decoded = jnp.dot(code, dec_weight, preferred_element_type=jnp.float32).astype(jnp.bfloat16)
    arrived = lax.all_to_all(decoded, "dict", split_axis=1, concat_axis=0, tiled=True)
    placed = jnp.where(valid_all.reshape(-1)[:, None], arrived.astype(jnp.float32), 0.0)
    recon = jnp.zeros((tok_rows, feat_dev), jnp.float32).at[rows_all].add(placed)
    skip = jnp.dot(whole, skip_weight, preferred_element_type=jnp.float32)
    err = recon + skip + dec_bias[None, :] - target.astype(jnp.float32)
    grad_out = (err * scale).astype(jnp.bfloat16)
    outgoing = grad_out[rows_all]
    grad_rows = lax.all_to_all(outgoing, "dict", split_axis=0, concat_axis=1, tiled=True)
    back = lax.dot_general(
        grad_rows, dec_weight, (((1,), (1,)), ((), ())), preferred_element_type=jnp.float32
    )
    dpre = jnp.where(active, back * slope, 0.0).astype(jnp.bfloat16)
    enc_term = lax.dot_general(
        picked, dpre, (((0,), (0,)), ((), ())), preferred_element_type=jnp.float32
    )
    dec_term = lax.dot_general(
        code, grad_rows, (((0,), (0,)), ((), ())), preferred_element_type=jnp.float32
    )
    skip_term = lax.dot_general(
        whole, grad_out, (((0,), (0,)), ((), ())), preferred_element_type=jnp.float32
    )
    grad_enc, grad_dec, grad_skip = (
        lax.psum_scatter(
            enc_term.astype(jnp.bfloat16), "tok", scatter_dimension=0, tiled=True
        ).astype(jnp.float32),
        lax.psum_scatter(
            dec_term.astype(jnp.bfloat16), "tok", scatter_dimension=1, tiled=True
        ).astype(jnp.float32),
        lax.psum_scatter(
            skip_term.astype(jnp.bfloat16), "tok", scatter_dimension=0, tiled=True
        ).astype(jnp.float32),
    )
    return (grad_enc, grad_dec, grad_skip)


def solution(mesh):
    in_specs = (
        P("tok", "dict"),
        P("tok", "dict"),
        P(None, "dict"),
        P("dict"),
        P("dict", None),
        P("dict"),
        P(None, "dict"),
        P("tok", None),
        P("tok", None, None),
        P("tok", None),
    )
    out_specs = (P("tok", "dict"), P("dict", "tok"), P("tok", "dict"))
    return jax.shard_map(local, mesh=mesh, in_specs=in_specs, out_specs=out_specs, check_vma=False)
```

profile of v0, /device:TPU:8, one launch (start us, length us, event | category | flops | bytes accessed | tf_op | source)
XLA Modules:
  0.0 460.9 jit_solution(1945707312323721416)
XLA Ops:
  11.6 149.3 %all-gather.2.cloned.1.call-done = bf16[512,4608]{0,1:T(8,128)(2,1)} async-done(((bf16[512,72]{0,1:T(8,128)(2,1)}), bf16[512,4608]{0,1:T(8,128)(2,1)}) %all-gather.2.cloned.1.call-update) | async-done | bytes 4718608 | tf_op jit(solution)/shard_map/all_gather | solution.py:40
  160.9 6.7 %copy.30 = bf16[512,4608]{1,0:T(8,128)(2,1)} copy(bf16[512,4608]{0,1:T(8,128)(2,1)} %all-gather.2.cloned.1.call-done) | data formatting | bytes 9437184 | tf_op jit(solution)/shard_map/all_gather | solution.py:40
  167.6 5.0 %gather_fusion = bf16[96,4608]{1,0:T(8,128)(2,1)S(1)} fusion(bf16[512,4608]{1,0:T(8,128)(2,1)} %copy.30, s32[1024]{0:T(1024)S(1)} %get-tuple-element.6), kind=kCustom, calls=%fused_computation | custom fusion | bytes 1769856 | tf_op jit(solution)/shard_map/gather | solution.py:51
  174.9 11.3 %all-to-all-start = ((bf16[96,64,72]{0,2,1:T(8,128)(2,1)}), bf16[96,64,72]{0,2,1:T(8,128)(2,1)}, u32[]{:S(2)}, u32[]{:S(2)}) async-start(bf16[96,64,72]{0,2,1:T(8,128)(2,1)} %bitcast.6), calls=%async_computation | async-start | bytes 2359296 | tf_op jit(solution)/shard_map/all_to_all | solution.py:56
  186.7 3.3 convolution_add_fusion
  190.1 48.1 %all-to-all-done = bf16[96,64,72]{0,2,1:T(8,128)(2,1)} async-done(((bf16[96,64,72]{0,2,1:T(8,128)(2,1)}), bf16[96,64,72]{0,2,1:T(8,128)(2,1)}, u32[]{:S(2)}, u32[]{:S(2)}) %all-to-all-start) | async-done | bytes 884768 | tf_op jit(solution)/shard_map/all_to_all | solution.py:56
  238.2 1.4 convert_bitcast_fusion
  239.6 1.9 copy.33
  241.5 3.7 reshape.259
  245.2 2.9 broadcast_select_fusion
  248.1 3.3 copy.35
  251.4 38.6 %scatter_fusion = f32[512,72]{1,0:T(8,128)S(1)} fusion(f32[512,72]{1,0:T(8,128)S(1)} %copy.34, s32[6144]{0:T(1024)S(1)} %bitcast.46, f32[6144,72]{1,0:T(8,128)} %copy.35), kind=kCustom, calls=%fused_computation.3 | custom fusion | flops 442368 | bytes 5332992 | tf_op jit(solution)/shard_map/scatter-add | solution.py:58
  290.0 22.1 %gather_fusion.2 = bf16[6144,72]{1,0:T(8,128)(2,1)} fusion(bf16[512,72]{1,0:T(8,128)(2,1)S(1)} %multiply_convert_fusion, s32[6144]{0:T(1024)S(1)} %broadcast_clamp_fusion), kind=kCustom, calls=%fused_computation.2 | custom fusion | bytes 1794048 | tf_op jit(solution)/shard_map/gather | solution.py:62
  312.1 2.5 copy.37
  314.6 6.0 %all-to-all-start.1 = ((bf16[64,96,72]{1,2,0:T(8,128)(2,1)}), bf16[64,96,72]{1,2,0:T(8,128)(2,1)S(1)}, u32[]{:S(2)}, u32[]{:S(2)}) async-start(bf16[64,96,72]{1,2,0:T(8,128)(2,1)} %copy.37), calls=%async_computation.1 | async-start | bytes 2359296 | tf_op jit(solution)/shard_map/all_to_all | solution.py:63
  320.6 4.7 %fusion = bf16[4608,72]{0,1:T(8,128)(2,1)} fusion(bf16[512,72]{1,0:T(8,128)(2,1)S(1)} %multiply_convert_fusion, bf16[512,4608]{0,1:T(8,128)(2,1)} %all-gather.2.cloned.1.call-done), kind=kOutput, calls=%fused_computation.8 | convolution fusion | flops 340070400 | bytes 5455872 | tf_op jit(solution)/shard_map/dot_general | solution.py:74
  325.3 2.3 copy.38
  327.7 48.9 %all-to-all-done.1 = bf16[64,96,72]{1,2,0:T(8,128)(2,1)S(1)} async-done(((bf16[64,96,72]{1,2,0:T(8,128)(2,1)}), bf16[64,96,72]{1,2,0:T(8,128)(2,1)S(1)}, u32[]{:S(2)}, u32[]{:S(2)}) %all-to-all-start.1) | async-done | bytes 884768 | tf_op jit(solution)/shard_map/all_to_all | solution.py:63
  376.6 1.6 convolution_convert_fusion
  378.2 2.5 convolution_convert_fusion.1
  382.5 28.5 %reduce-scatter.8.cloned.1.call-done = bf16[128,576]{0,1:T(8,128)(2,1)} async-done(((bf16[128,4608]{0,1:T(8,128)(2,1)}), bf16[128,576]{0,1:T(8,128)(2,1)}) %reduce-scatter.8.cloned.1.call-update) | async-done | bytes 147472 | tf_op jit(solution)/shard_map/reduce_scatter | solution.py:81
  411.0 1.6 convert_element_type.56
  412.7 40.0 %reduce-scatter.6.cloned.1.call-done = bf16[576,128]{1,0:T(8,128)(2,1)} async-done(((bf16[4608,128]{1,0:T(8,128)(2,1)}), bf16[576,128]{1,0:T(8,128)(2,1)}) %reduce-scatter.6.cloned.1.call-update) | async-done | bytes 147472 | tf_op jit(solution)/shard_map/reduce_scatter | solution.py:78
  452.7 1.6 convert_element_type.54
  (43 shorter events, 9.2 us)
Async XLA Ops:
  7.2 165.9 %copy-start = (bf16[128,4608]{1,0:T(8,128)(2,1)S(1)}, bf16[128,4608]{1,0:T(8,128)(2,1)}, u32[]{:S(2)}) copy-start(bf16[128,4608]{1,0:T(8,128)(2,1)} %param.14) | copy-start | bytes 3538948
  7.2 153.7 %all-gather.2.cloned.1.call-start = ((), (), s32[]{:S(2)}) async-start(), calls=%async_computation.5 | async-start | bytes 4792320 | tf_op jit(solution)/shard_map/all_gather | solution.py:40
  167.6 5.0 %copy-start.1 = (bf16[4608,128]{1,0:T(8,128)(2,1)S(1)}, bf16[4608,128]{1,0:T(8,128)(2,1)}, u32[]{:S(2)}) copy-start(bf16[4608,128]{1,0:T(8,128)(2,1)} %param.12) | copy-start | bytes 3538948
  167.6 5.0 %copy-start.6 = (f32[128]{0:T(128)S(1)}, f32[128]{0:T(128)}, u32[]{:S(2)}) copy-start(f32[128]{0:T(128)} %param.13) | copy-start | bytes 1540
  174.9 11.4 %copy-start.4 = (s32[1,64,96]{2,1,0:T(8,128)S(1)}, s32[1,64,96]{2,1,0:T(8,128)}, u32[]{:S(2)}) copy-start(s32[1,64,96]{2,1,0:T(8,128)} %param.18) | copy-start | bytes 73732
  174.9 11.5 %copy-start.3 = (bf16[512,72]{0,1:T(8,128)(2,1)S(1)}, bf16[512,72]{0,1:T(8,128)(2,1)}, u32[]{:S(2)}) copy-start(bf16[512,72]{0,1:T(8,128)(2,1)} %param.11) | copy-start | bytes 221188
  174.9 11.8 %copy-start.2 = (bf16[4608,72]{0,1:T(8,128)(2,1)S(1)}, bf16[4608,72]{0,1:T(8,128)(2,1)}, u32[]{:S(2)}) copy-start(bf16[4608,72]{0,1:T(8,128)(2,1)} %param.16) | copy-start | bytes 1990660
  174.9 11.8 %copy-start.5 = (f32[72]{0:T(128)S(1)}, f32[72]{0:T(128)}, u32[]{:S(2)}) copy-start(f32[72]{0:T(128)} %param.15) | copy-start | bytes 868
  174.9 63.3 %all-to-all-start = ((bf16[96,64,72]{0,2,1:T(8,128)(2,1)}), bf16[96,64,72]{0,2,1:T(8,128)(2,1)}, u32[]{:S(2)}, u32[]{:S(2)}) async-start(bf16[96,64,72]{0,2,1:T(8,128)(2,1)} %bitcast.6), calls=%async_computation | async-start | bytes 2359296 | tf_op jit(solution)/shard_map/all_to_all | solution.py:56
  314.6 62.0 %all-to-all-start.1 = ((bf16[64,96,72]{1,2,0:T(8,128)(2,1)}), bf16[64,96,72]{1,2,0:T(8,128)(2,1)S(1)}, u32[]{:S(2)}, u32[]{:S(2)}) async-start(bf16[64,96,72]{1,2,0:T(8,128)(2,1)} %copy.37), calls=%async_computation.1 | async-start | bytes 2359296 | tf_op jit(solution)/shard_map/all_to_all | solution.py:63
  320.6 60.2 %reduce-scatter.10.cloned.1.call-start = ((), (), s32[]{:S(2)}) async-start(), calls=%async_computation.8 | async-start | bytes 1327104
  327.7 83.4 %reduce-scatter.8.cloned.1.call-start = ((), (), s32[]{:S(2)}) async-start(), calls=%async_computation.7 | async-start | bytes 1327104 | tf_op jit(solution)/shard_map/reduce_scatter | solution.py:81
  378.2 74.5 %reduce-scatter.6.cloned.1.call-start = ((), (), s32[]{:S(2)}) async-start(), calls=%async_computation.6 | async-start | bytes 1327104 | tf_op jit(solution)/shard_map/reduce_scatter | solution.py:78
Sparse Core Ops, SparseCore 0:
  10.9 149.9 all-gather.1
  327.8 41.3 reduce-scatter.9
  378.3 32.7 reduce-scatter.7
  413.7 38.9 reduce-scatter.5
where the time goes:
time: 462 us; the launch traced here: 461 us
  waiting for transfers between devices  316 us (68%)
  local copies, waits for them, and re-layouts  52.4 us (11%)
  other arithmetic  48.6 us (11%)
  starting transfers between devices  17.4 us (4%)
  between operations  14 us (3%)
  matrix products  12.9 us (3%)
    all_gather x1, waiting for transfers between devices, local(): whole = lax.all_gather(inputs, 'dict', axis=1, tiled=True)  149 us
    all_to_all x1, waiting for transfers between devices, local(): lax.all_to_all(outgoing, 'dict', split_axis=0, concat_axis=1, tiled=True)  48.9 us
    all_to_all x1, waiting for transfers between devices, local(): lax.all_to_all(decoded, 'dict', split_axis=1, concat_axis=0, tiled=True)  48.1 us
    reduce_scatter x1, waiting for transfers between devices, local(): lax.psum_scatter(enc_term.astype(jnp.bfloat16), 'tok', scatter_dimension=...  40 us
    scatter-add x1, other arithmetic, local(): jnp.zeros((tok_rows, feat_dev), jnp.float32).at[rows_all].add(placed)  38.6 us
    reduce_scatter x1, waiting for transfers between devices, local(): lax.psum_scatter(dec_term.astype(jnp.bfloat16), 'tok', scatter_dimension=...  28.5 us
    gather x1, local copies, waits for them, and re-layouts, local(): outgoing = grad_out[rows_all]  22.1 us
    all_to_all x1, starting transfers between devices, local(): lax.all_to_all(decoded, 'dict', split_axis=1, concat_axis=0, tiled=True)  11.3 us
  transfers between devices with their start and end apart: 6, of which 5 were waited for; matrix products, arithmetic and copies ran while one was open for 5% of the time, Pallas kernels for 0%

commit v1 on v0

v1 whole, which is shorter than its diff:
```python
import math

import jax
import jax.numpy as jnp
from jax import lax
from jax.sharding import Mesh
from jax.sharding import PartitionSpec as P

BLK = 16
NY = 4
TOK = ("x", "core")
DICT = ("z", "y")
bf16 = jnp.bfloat16
f32 = jnp.float32


def gelu_pair(pre):
    factor = math.sqrt(2.0 / math.pi)
    inner = jnp.tanh(factor * (pre + 0.044715 * pre * pre * pre))
    value = 0.5 * pre * (1.0 + inner)
    slope = 0.5 * (1.0 + inner) + 0.5 * pre * (1.0 - inner * inner) * factor * (
        1.0 + 3.0 * 0.044715 * pre * pre
    )
    return (value, slope)


def ein(spec, a, b):
    return jnp.einsum(spec, a, b, preferred_element_type=f32)


def pick_plan(slots, counts, blocks_t, tok_rows, nb):
    per_token = blocks_t.shape[0]
    cap = slots.shape[1]
    token = slots // per_token
    hot = (token[:, :, None] == jnp.arange(tok_rows, dtype=jnp.int32)).astype(bf16)
    named = ein("rt,nst->nrs", (blocks_t % nb).astype(bf16), hot)
    rank = (slots % per_token)[:, None, :] == jnp.arange(per_token, dtype=jnp.int32)[None, :, None]
    block = jnp.sum(jnp.where(rank, named, 0.0), axis=1)
    valid = jnp.arange(cap, dtype=jnp.int32)[None, :] < counts[:, None]
    mask = (block[:, None, :] == jnp.arange(nb, dtype=f32)[None, :, None]) & valid[:, None, :]
    return hot, mask


def compress(part, plan):
    hot, mask = plan
    n, nb, cap = mask.shape
    rows = ein("nlt,nst->nls", part, hot).reshape(n, nb, BLK, cap)
    return jnp.sum(jnp.where(mask[:, :, None, :], rows, 0.0), axis=1)


def expand(slot_vals, plan):
    hot, mask = plan
    n, nb, cap = mask.shape
    rows = jnp.where(mask[:, :, None, :], slot_vals[:, None, :, :], jnp.zeros((), bf16))
    return ein("nls,nst->nlt", rows.reshape(n, nb * BLK, cap), hot).astype(bf16)


def local(
    inputs,
    target,
    enc_weight,
    enc_bias,
    dec_weight,
    dec_bias,
    skip_weight,
    block_ids,
    slot_lists,
    slot_counts,
):
    tok_rows, fd = inputs.shape
    ld = enc_weight.shape[1]
    nz, ny = lax.axis_size("z"), lax.axis_size("y")
    nx, nc = lax.axis_size("x"), lax.axis_size("core")
    nt = nx * nc
    zl = nz // nt
    nb = ld // BLK
    cap = slot_lists.shape[2]
    zi, yi, ci = lax.axis_index("z"), lax.axis_index("y"), lax.axis_index("core")
    scale = 1.0 / math.sqrt(tok_rows * nt)
    xt = inputs.T
    tt = target.T
    xq = lax.all_gather(xt, "z", axis=0, tiled=True)
    er = lax.all_to_all(enc_weight.reshape(nz, ny, fd, ld), "y", 1, 0).reshape(ny, nz * fd, ld)
    wr = lax.all_to_all(skip_weight.reshape(nz, ny, fd, fd), "y", 1, 0).reshape(ny, nz * fd, fd)
    half = ny * fd // nc
    dt = dec_weight.T.reshape(nz, nc, half, ld)
    dt = lax.dynamic_index_in_dim(dt, ci, 1, keepdims=False)
    dt = lax.all_to_all(dt, "z", 0, 0)
    dd = jnp.concatenate(
        [lax.all_gather(dt[: nz // 2], "core"), lax.all_gather(dt[nz // 2 :], "core")], axis=1
    )
    blocks_t = block_ids.T
    slots = slot_lists[0].reshape(nz, ny, cap)
    counts = slot_counts[0].reshape(nz, ny)
    plan_l = pick_plan(
        lax.dynamic_index_in_dim(slots, yi, 1, keepdims=False),
        lax.dynamic_index_in_dim(counts, yi, 1, keepdims=False),
        blocks_t, tok_rows, nb,
    )
    plan_z = pick_plan(
        lax.dynamic_index_in_dim(slots, zi, 0, keepdims=False),
        lax.dynamic_index_in_dim(counts, zi, 0, keepdims=False),
        blocks_t, tok_rows, nb,
    )
    own_mask = lax.dynamic_index_in_dim(plan_z[1], yi, 0, keepdims=False)
    bias = jnp.sum(jnp.where(own_mask[:, None, :], enc_bias.reshape(nb, BLK)[:, :, None], 0.0), axis=0)
    pre_part = ein("yrl,rt->ylt", er, xq).astype(bf16)
    pre_slots = lax.all_to_all(compress(pre_part, plan_z), "y", 0, 0)
    pre = jnp.sum(pre_slots, axis=0) + bias
    value, slope = gelu_pair(pre)
    code = value.astype(bf16)
    codes_l = lax.all_to_all(jnp.broadcast_to(code[None], (nz,) + code.shape), "z", 0, 0)
    codes_z = lax.all_gather(code, "y")
    dense_l = expand(codes_l, plan_l)
    recon = ein("hzfl,zlt->hft", dd, dense_l).reshape(ny, fd, tok_rows)
    skip = ein("yrc,rt->yct", wr, xq)
    out_part = lax.all_to_all((recon + skip).astype(bf16), "y", 0, 0)
    err = jnp.sum(out_part.astype(f32), axis=0) + dec_bias[:, None] - tt.astype(f32)
    grad = (err * scale).astype(bf16)
    gq = lax.all_gather(grad, "z", axis=0, tiled=True)
    gz = lax.all_gather(grad, "y", axis=0, tiled=True)
    back_part = ein("hzfl,hft->zlt", dd, gz.reshape(nc, half, tok_rows)).astype(bf16)
    back_slots = lax.all_to_all(compress(back_part, plan_l).astype(bf16), "z", 0, 0)
    back = jnp.sum(back_slots.astype(f32), axis=0)
    dpre = (back * slope).astype(bf16)
    dpre_z = expand(lax.all_gather(dpre, "y"), plan_z).reshape(ny * ld, tok_rows)
    code_z = expand(codes_z, plan_z).reshape(ny * ld, tok_rows)
    skip_term = ein("rt,ct->rc", xq, gz).astype(bf16)
    enc_term = ein("rt,lt->rl", xq, dpre_z).astype(bf16)
    dec_term = ein("rt,lt->rl", gq, code_z).astype(bf16)

    def reduce_tok(term):
        c = term.shape[1]
        parts = term.reshape(nx, nc, zl * fd, c)
        mine = lax.dynamic_index_in_dim(parts, ci, 1, keepdims=False)
        theirs = lax.dynamic_index_in_dim(parts, 1 - ci, 1, keepdims=False)
        got = lax.ppermute(theirs, "core", [(0, 1), (1, 0)])
        pair = (mine.astype(f32) + got.astype(f32)).astype(bf16)
        moved = lax.all_to_all(pair, "x", 0, 0)
        return jnp.sum(moved.astype(f32), axis=0)

    def to_owner(total, width):
        t = total.astype(bf16).reshape(zl * fd, ny, width).transpose(1, 0, 2)
        t = lax.all_to_all(t, "y", 0, 0).reshape(ny, zl, fd, width)
        return t.transpose(1, 0, 2, 3).reshape(zl * ny * fd, width).astype(f32)

    grad_skip = to_owner(reduce_tok(skip_term), fd)
    grad_enc = to_owner(reduce_tok(enc_term), ld)
    grad_dec = to_owner(reduce_tok(dec_term), ld).T
    return (grad_enc, grad_dec, grad_skip)


def solution(mesh):
    nt, nd = mesh.devices.shape
    grid = Mesh(mesh.devices.reshape(nt // 2, 2, nd // NY, NY), ("x", "core", "z", "y"))
    in_specs = (
        P(TOK, DICT),
        P(TOK, DICT),
        P(None, DICT),
        P(DICT),
        P(DICT, None),
        P(DICT),
        P(None, DICT),
        P(TOK, None),
        P(TOK, None, None),
        P(TOK, None),
    )
    out_specs = (P(TOK, DICT), P(DICT, TOK), P(TOK, DICT))
    return jax.shard_map(local, mesh=grid, in_specs=in_specs, out_specs=out_specs, check_vma=False)
```

time: 462 us -> 323 us (0.70)
  the two profiles are of different devices: /device:TPU:8 before, /device:TPU:32 now
where the time goes in v1:
time: 323 us; the launch traced here: 321 us
  waiting for transfers between devices  138 us (43%)
  starting transfers between devices  74.4 us (23%)
  blocking collectives  41.2 us (13%)
  local copies, waits for them, and re-layouts  22.6 us (7%)
  matrix products  17.4 us (5%)
  between operations  14.5 us (4%)
  other arithmetic  12.3 us (4%)
    all_gather x1, waiting for transfers between devices, local(): xq = lax.all_gather(xt, 'z', axis=0, tiled=True)  52.9 us
    all_to_all x3, waiting for transfers between devices, reduce_tok(): moved = lax.all_to_all(pair, 'x', 0, 0)  18.4 us
    dot_general x11, matrix products, ein(): return jnp.einsum(spec, a, b, preferred_element_type=f32)  17.4 us
    all_to_all x1, waiting for transfers between devices, local(): lax.all_to_all(skip_weight.reshape(nz, ny, fd, fd), 'y', 1, 0)  15.4 us
    all_to_all x1, starting transfers between devices, local(): dt = lax.all_to_all(dt, 'z', 0, 0)  15.2 us
    all_to_all x3, waiting for transfers between devices, to_owner(): t = lax.all_to_all(t, 'y', 0, 0).reshape(ny, zl, fd, width)  13.3 us
    all_gather x1, blocking collectives, local(): gz = lax.all_gather(grad, 'y', axis=0, tiled=True)  12.7 us
    all_gather x1, blocking collectives, local(): codes_z = lax.all_gather(code, 'y')  12 us
  transfers between devices with their start and end apart: 18, of which 13 were waited for; matrix products, arithmetic and copies ran while one was open for 12% of the time, Pallas kernels for 0%

profile of v1, /device:TPU:32, one launch (start us, length us, event | category | flops | bytes accessed | tf_op | source)
XLA Modules:
  0.0 320.8 jit_solution(1820733823230319644)
XLA Ops:
  7.2 5.3 %broadcast_in_dim_reshape.8 = bf16[1,16,4,72,72]{3,2,1,4,0:T(4,128)(2,1)S(1)} reshape(bf16[4608,72]{0,1:T(8,128)(2,1)} %param.16) | data formatting | bytes 1327104 | tf_op jit(solution)/shard_map/broadcast_in_dim;reshape | solution.py:84
  13.6 4.6 %all-to-all-start.4 = ((bf16[1,16,4,72,72]{3,1,4,0,2:T(8,128)(2,1)}), bf16[1,16,4,72,72]{3,1,4,0,2:T(8,128)(2,1)S(1)}, u32[]{:S(2)}, u32[]{:S(2)}) async-start(bf16[1,16,4,72,72]{3,1,4,0,2:T(8,128)(2,1)} %copy.84), calls=%async_computation.4 | async-start | bytes 2359296 | tf_op jit(solution)/shard_map/all_to_all | solution.py:84
  19.4 15.4 %all-to-all-done.4 = bf16[1,16,4,72,72]{3,1,4,0,2:T(8,128)(2,1)S(1)} async-done(((bf16[1,16,4,72,72]{3,1,4,0,2:T(8,128)(2,1)}), bf16[1,16,4,72,72]{3,1,4,0,2:T(8,128)(2,1)S(1)}, u32[]{:S(2)}, u32[]{:S(2)}) %all-to-all-start.4) | async-done | bytes 663584 | tf_op jit(solution)/shard_map/all_to_all | solution.py:84
  34.7 4.3 %all-to-all-start.1 = ((bf16[1,16,4,72,128]{4,3,1,0,2:T(8,128)(2,1)}), bf16[1,16,4,72,128]{4,3,1,0,2:T(8,128)(2,1)}, u32[]{:S(2)}, u32[]{:S(2)}) async-start(bf16[1,16,4,72,128]{4,3,1,0,2:T(8,128)(2,1)} %copy.80), calls=%async_computation.1 | async-start | bytes 2359296 | tf_op jit(solution)/shard_map/all_to_all | solution.py:83
  45.1 9.6 %all-to-all-done.1 = bf16[1,16,4,72,128]{4,3,1,0,2:T(8,128)(2,1)} async-done(((bf16[1,16,4,72,128]{4,3,1,0,2:T(8,128)(2,1)}), bf16[1,16,4,72,128]{4,3,1,0,2:T(8,128)(2,1)}, u32[]{:S(2)}, u32[]{:S(2)}) %all-to-all-start.1) | async-done | bytes 1179680 | tf_op jit(solution)/shard_map/all_to_all | solution.py:83
  54.7 15.2 %all-to-all-start = ((bf16[16,144,128]{2,1,0:T(8,128)(2,1)}), bf16[16,144,128]{2,1,0:T(8,128)(2,1)S(1)}, u32[]{:S(2)}, u32[]{:S(2)}) async-start(bf16[16,144,128]{2,1,0:T(8,128)(2,1)} %dynamic-slice_bitcast_fusion.2), calls=%async_computation | async-start | bytes 1179648 | tf_op jit(solution)/shard_map/all_to_all | solution.py:88
  73.9 52.9 %all-gather.5.cloned.1.call-done = bf16[1152,512]{1,0:T(8,128)(2,1)} async-done(((bf16[72,512]{1,0:T(8,128)(2,1)}), bf16[1152,512]{1,0:T(8,128)(2,1)}) %all-gather.5.cloned.1.call-update) | async-done | bytes 1179664 | tf_op jit(solution)/shard_map/all_gather | solution.py:82
  130.1 5.5 %all-to-all-start.2 = ((f32[4,16,96]{2,1,0:T(8,128)}), f32[4,16,96]{2,1,0:T(8,128)S(1)}, u32[]{:S(2)}, u32[]{:S(2)}) async-start(f32[4,16,96]{2,1,0:T(8,128)} %select_reduce_fusion.1), calls=%async_computation.2 | async-start | bytes 65536 | tf_op jit(solution)/shard_map/all_to_all | solution.py:108
  135.6 5.4 %all-to-all-done.2 = f32[4,16,96]{2,1,0:T(8,128)S(1)} async-done(((f32[4,16,96]{2,1,0:T(8,128)}), f32[4,16,96]{2,1,0:T(8,128)S(1)}, u32[]{:S(2)}, u32[]{:S(2)}) %all-to-all-start.2) | async-done | bytes 24608 | tf_op jit(solution)/shard_map/all_to_all | solution.py:108
  141.6 8.5 %all-to-all-start.3 = ((bf16[16,16,96]{2,1,0:T(8,128)(2,1)}), bf16[16,16,96]{2,1,0:T(8,128)(2,1)S(1)}, u32[]{:S(2)}, u32[]{:S(2)}) async-start(bf16[16,16,96]{2,1,0:T(8,128)(2,1)} %broadcast_in_dim.145), calls=%async_computation.3 | async-start | bytes 131072 | tf_op jit(solution)/shard_map/all_to_all | solution.py:112
  154.6 7.4 %all-to-all-done.3 = bf16[16,16,96]{2,1,0:T(8,128)(2,1)S(1)} async-done(((bf16[16,16,96]{2,1,0:T(8,128)(2,1)}), bf16[16,16,96]{2,1,0:T(8,128)(2,1)S(1)}, u32[]{:S(2)}, u32[]{:S(2)}) %all-to-all-start.3) | async-done | bytes 49184 | tf_op jit(solution)/shard_map/all_to_all | solution.py:112
  171.2 7.1 %all-to-all-done.5 = bf16[4,72,512]{2,1,0:T(8,128)(2,1)S(1)} async-done(((bf16[4,72,512]{2,1,0:T(8,128)(2,1)}), bf16[4,72,512]{2,1,0:T(8,128)(2,1)S(1)}, u32[]{:S(2)}, u32[]{:S(2)}) %all-to-all-start.5) | async-done | bytes 294944 | tf_op jit(solution)/shard_map/all_to_all | solution.py:117
  179.1 12.7 %all_gather.34 = bf16[288,512]{1,0:T(8,128)(2,1)S(1)} all-gather(bf16[72,512]{1,0:T(8,128)(2,1)} %fusion.30), channel_id=1, replica_groups=mesh['x'=4,'core'=2,'z'=16,'y'=4] {'y'}, dimensions={0}, use_global_device_ids=true | all-gather | bytes 368640 | tf_op jit(solution)/shard_map/all_gather | solution.py:121
  195.7 5.4 %all-to-all-start.6 = ((bf16[16,16,96]{2,1,0:T(8,128)(2,1)}), bf16[16,16,96]{2,1,0:T(8,128)(2,1)S(1)}, u32[]{:S(2)}, u32[]{:S(2)}) async-start(bf16[16,16,96]{2,1,0:T(8,128)(2,1)} %select_reduce_fusion), calls=%async_computation.6 | async-start | bytes 131072 | tf_op jit(solution)/shard_map/all_to_all | solution.py:123
  204.9 8.3 %all-to-all-done.6 = bf16[16,16,96]{2,1,0:T(8,128)(2,1)S(1)} async-done(((bf16[16,16,96]{2,1,0:T(8,128)(2,1)}), bf16[16,16,96]{2,1,0:T(8,128)(2,1)S(1)}, u32[]{:S(2)}, u32[]{:S(2)}) %all-to-all-start.6) | async-done | bytes 49184 | tf_op jit(solution)/shard_map/all_to_all | solution.py:123
  213.2 12.0 %all_gather.37 = bf16[4,16,96]{2,1,0:T(8,128)(2,1)S(1)} all-gather(bf16[1,16,96]{2,1,0:T(8,128)(2,1)S(1)} %get-tuple-element.7), channel_id=1, replica_groups=mesh['x'=4,'core'=2,'z'=16,'y'=4] {'y'}, dimensions={0}, use_global_device_ids=true | all-gather | bytes 15360 | tf_op jit(solution)/shard_map/all_gather | solution.py:113
  225.2 12.0 %all_gather.35 = bf16[4,16,96]{2,1,0:T(8,128)(2,1)S(1)} all-gather(bf16[1,16,96]{2,1,0:T(8,128)(2,1)S(1)} %get-tuple-element.8), channel_id=1, replica_groups=mesh['x'=4,'core'=2,'z'=16,'y'=4] {'y'}, dimensions={0}, use_global_device_ids=true | all-gather | bytes 15360 | tf_op jit(solution)/shard_map/all_gather | solution.py:126
  244.9 4.3 %all-to-all-start.11 = ((bf16[4,144,288]{2,1,0:T(8,128)(2,1)}), bf16[4,144,288]{2,1,0:T(8,128)(2,1)S(1)}, u32[]{:S(2)}, u32[]{:S(2)}) async-start(bf16[4,144,288]{2,1,0:T(8,128)(2,1)} %fusion.24), calls=%async_computation.11 | async-start | bytes 884736 | tf_op jit(solution)/shard_map/all_to_all | solution.py:139
  254.5 4.0 %all-to-all-done.11 = bf16[4,144,288]{2,1,0:T(8,128)(2,1)S(1)} async-done(((bf16[4,144,288]{2,1,0:T(8,128)(2,1)}), bf16[4,144,288]{2,1,0:T(8,128)(2,1)S(1)}, u32[]{:S(2)}, u32[]{:S(2)}) %all-to-all-start.11) | async-done | bytes 331808 | tf_op jit(solution)/shard_map/all_to_all | solution.py:139
  266.4 4.0 %all-to-all-done.12 = bf16[4,144,72]{2,1,0:T(8,128)(2,1)S(1)} async-done(((bf16[4,144,72]{2,1,0:T(8,128)(2,1)}), bf16[4,144,72]{2,1,0:T(8,128)(2,1)S(1)}, u32[]{:S(2)}, u32[]{:S(2)}) %all-to-all-start.12) | async-done | bytes 82976 | tf_op jit(solution)/shard_map/all_to_all | solution.py:144
  275.9 6.8 %all-to-all-done.7 = bf16[4,144,512]{2,1,0:T(8,128)(2,1)S(1)} async-done(((bf16[4,144,512]{2,1,0:T(8,128)(2,1)}), bf16[4,144,512]{2,1,0:T(8,128)(2,1)S(1)}, u32[]{:S(2)}, u32[]{:S(2)}) %all-to-all-start.7) | async-done | bytes 589856 | tf_op jit(solution)/shard_map/all_to_all | solution.py:139
  286.9 7.6 %all-to-all-done.9 = bf16[4,144,512]{2,1,0:T(8,128)(2,1)S(1)} async-done(((bf16[4,144,512]{2,1,0:T(8,128)(2,1)}), bf16[4,144,512]{2,1,0:T(8,128)(2,1)S(1)}, u32[]{:S(2)}, u32[]{:S(2)}) %all-to-all-start.9) | async-done | bytes 589856 | tf_op jit(solution)/shard_map/all_to_all | solution.py:139
  299.7 4.1 %all-to-all-done.8 = bf16[4,144,128]{2,1,0:T(8,128)(2,1)S(1)} async-done(((bf16[4,144,128]{2,1,0:T(8,128)(2,1)}), bf16[4,144,128]{2,1,0:T(8,128)(2,1)S(1)}, u32[]{:S(2)}, u32[]{:S(2)}) %all-to-all-start.8) | async-done | bytes 147488 | tf_op jit(solution)/shard_map/all_to_all | solution.py:144
  308.0 5.3 %all-to-all-done.10 = bf16[4,144,128]{2,1,0:T(8,128)(2,1)S(1)} async-done(((bf16[4,144,128]{2,1,0:T(8,128)(2,1)}), bf16[4,144,128]{2,1,0:T(8,128)(2,1)S(1)}, u32[]{:S(2)}, u32[]{:S(2)}) %all-to-all-start.10) | async-done | bytes 147488 | tf_op jit(solution)/shard_map/all_to_all | solution.py:144
  (134 shorter events, 78.7 us)
Async XLA Ops:
  13.6 21.1 %all-to-all-start.4 = ((bf16[1,16,4,72,72]{3,1,4,0,2:T(8,128)(2,1)}), bf16[1,16,4,72,72]{3,1,4,0,2:T(8,128)(2,1)S(1)}, u32[]{:S(2)}, u32[]{:S(2)}) async-start(bf16[1,16,4,72,72]{3,1,4,0,2:T(8,128)(2,1)} %copy.84), calls=%async_computation.4 | async-start | bytes 2359296 | tf_op jit(solution)/shard_map/all_to_all | solution.py:84
  34.7 20.0 %all-to-all-start.1 = ((bf16[1,16,4,72,128]{4,3,1,0,2:T(8,128)(2,1)}), bf16[1,16,4,72,128]{4,3,1,0,2:T(8,128)(2,1)}, u32[]{:S(2)}, u32[]{:S(2)}) async-start(bf16[1,16,4,72,128]{4,3,1,0,2:T(8,128)(2,1)} %copy.80), calls=%async_computation.1 | async-start | bytes 2359296 | tf_op jit(solution)/shard_map/all_to_all | solution.py:83
  39.0 87.7 %all-gather.5.cloned.1.call-start = ((), (), s32[]{:S(2)}) async-start(), calls=%async_computation.13 | async-start | bytes 1253376 | tf_op jit(solution)/shard_map/all_gather | solution.py:82
  43.8 82.9 %copy-start.12 = (s32[4,96]{1,0:T(4,128)}, s32[4,96]{1,0:T(4,128)S(1)}, u32[]{:S(2)}) copy-start(s32[4,96]{1,0:T(4,128)S(1)} %get-tuple-element.6) | copy-start | bytes 4612
  44.2 26.6 %copy-start.14 = (f32[8,16]{1,0:T(8,128)S(1)}, f32[8,16]{1,0:T(8,128)}, u32[]{:S(2)}) copy-start(f32[8,16]{1,0:T(8,128)} %broadcast_in_dim.142) | copy-start | bytes 1540
  44.2 26.7 %copy-start.20 = (s32[512,4]{0,1:T(4,128)S(1)}, s32[512,4]{0,1:T(4,128)}, u32[]{:S(2)}) copy-start(s32[512,4]{0,1:T(4,128)} %param.17) | copy-start | bytes 24580
  54.7 75.3 %all-to-all-start = ((bf16[16,144,128]{2,1,0:T(8,128)(2,1)}), bf16[16,144,128]{2,1,0:T(8,128)(2,1)S(1)}, u32[]{:S(2)}, u32[]{:S(2)}) async-start(bf16[16,144,128]{2,1,0:T(8,128)(2,1)} %dynamic-slice_bitcast_fusion.2), calls=%async_computation | async-start | bytes 1179648 | tf_op jit(solution)/shard_map/all_to_all | solution.py:88
  70.0 59.4 %copy-start.10 = (pred[4,8,96]{2,1,0:T(8,128)(4,1)}, pred[4,8,96]{2,1,0:T(8,128)(4,1)S(1)}, u32[]{:S(2)}) copy-start(pred[4,8,96]{2,1,0:T(8,128)(4,1)S(1)} %fusion.32) | copy-start | bytes 9220
  130.1 10.9 %all-to-all-start.2 = ((f32[4,16,96]{2,1,0:T(8,128)}), f32[4,16,96]{2,1,0:T(8,128)S(1)}, u32[]{:S(2)}, u32[]{:S(2)}) async-start(f32[4,16,96]{2,1,0:T(8,128)} %select_reduce_fusion.1), calls=%async_computation.2 | async-start | bytes 65536 | tf_op jit(solution)/shard_map/all_to_all | solution.py:108
  141.6 20.4 %all-to-all-start.3 = ((bf16[16,16,96]{2,1,0:T(8,128)(2,1)}), bf16[16,16,96]{2,1,0:T(8,128)(2,1)S(1)}, u32[]{:S(2)}, u32[]{:S(2)}) async-start(bf16[16,16,96]{2,1,0:T(8,128)(2,1)} %broadcast_in_dim.145), calls=%async_computation.3 | async-start | bytes 131072 | tf_op jit(solution)/shard_map/all_to_all | solution.py:112
  167.5 10.8 %all-to-all-start.5 = ((bf16[4,72,512]{2,1,0:T(8,128)(2,1)}), bf16[4,72,512]{2,1,0:T(8,128)(2,1)S(1)}, u32[]{:S(2)}, u32[]{:S(2)}) async-start(bf16[4,72,512]{2,1,0:T(8,128)(2,1)} %fusion.13), calls=%async_computation.5 | async-start | bytes 589824 | tf_op jit(solution)/shard_map/all_to_all | solution.py:117
  171.1 78.1 %all-gather.7.cloned.1.call-start = ((), (), s32[]{:S(2)}) async-start(), calls=%async_computation.14 | async-start | bytes 1253376 | tf_op jit(solution)/shard_map/all_gather | solution.py:120
  195.7 17.4 %all-to-all-start.6 = ((bf16[16,16,96]{2,1,0:T(8,128)(2,1)}), bf16[16,16,96]{2,1,0:T(8,128)(2,1)S(1)}, u32[]{:S(2)}, u32[]{:S(2)}) async-start(bf16[16,16,96]{2,1,0:T(8,128)(2,1)} %select_reduce_fusion), calls=%async_computation.6 | async-start | bytes 131072 | tf_op jit(solution)/shard_map/all_to_all | solution.py:123
  201.7 35.5 %copy-start.11 = (pred[4,8,96]{2,1,0:T(8,128)(4,1)S(1)}, pred[4,8,96]{2,1,0:T(8,128)(4,1)}, u32[]{:S(2)}) copy-start(pred[4,8,96]{2,1,0:T(8,128)(4,1)} %copy-done.10) | copy-start | bytes 9220
  201.7 36.2 %copy-start.13 = (s32[4,96]{1,0:T(4,128)S(1)}, s32[4,96]{1,0:T(4,128)}, u32[]{:S(2)}) copy-start(s32[4,96]{1,0:T(4,128)} %copy-done.12) | copy-start | bytes 4612
  202.9 40.1 %collective-permute-start.2 = (bf16[4,144,288]{2,1,0:T(8,128)(2,1)}, bf16[4,144,288]{2,1,0:T(8,128)(2,1)}, u32[]{:S(2)}, u32[]{:S(2)}) collective-permute-start(bf16[4,144,288]{2,1,0:T(8,128)(2,1)} %dynamic-slice_bitcast_fusion.3), channel_id=1, source_target_pairs={{0,64},{64,0},{1,65},{65,1},{2,66},{66,2},{3,67},{67,3},{4,68},{68... | collective-permute-start | bytes 995336 | tf_op jit(solution)/shard_map/ppermute | solution.py:137
  239.9 24.4 %collective-permute-start = (bf16[4,144,512]{2,1,0:T(8,128)(2,1)S(1)}, bf16[4,144,512]{2,1,0:T(8,128)(2,1)}, u32[]{:S(2)}, u32[]{:S(2)}) collective-permute-start(bf16[4,144,512]{2,1,0:T(8,128)(2,1)S(1)} %dynamic-slice_bitcast_fusion.1), channel_id=1, source_target_pairs={{0,64},{64,0},{1,65},{65,1},{2,66},{66,2},{3,67},{67,3},{4,68},{68... | collective-permute-start | bytes 1769480 | tf_op jit(solution)/shard_map/ppermute | solution.py:137
  244.9 13.6 %all-to-all-start.11 = ((bf16[4,144,288]{2,1,0:T(8,128)(2,1)}), bf16[4,144,288]{2,1,0:T(8,128)(2,1)S(1)}, u32[]{:S(2)}, u32[]{:S(2)}) async-start(bf16[4,144,288]{2,1,0:T(8,128)(2,1)} %fusion.24), calls=%async_computation.11 | async-start | bytes 884736 | tf_op jit(solution)/shard_map/all_to_all | solution.py:139
  252.3 21.5 %collective-permute-start.1 = (bf16[4,144,512]{2,1,0:T(8,128)(2,1)}, bf16[4,144,512]{2,1,0:T(8,128)(2,1)}, u32[]{:S(2)}, u32[]{:S(2)}) collective-permute-start(bf16[4,144,512]{2,1,0:T(8,128)(2,1)} %dynamic-slice_bitcast_fusion), channel_id=1, source_target_pairs={{0,64},{64,0},{1,65},{65,1},{2,66},{66,2},{3,67},{67,3},{4,68},{68... | collective-permute-start | bytes 1769480 | tf_op jit(solution)/shard_map/ppermute | solution.py:137
  261.0 9.4 %all-to-all-start.12 = ((bf16[4,144,72]{2,1,0:T(8,128)(2,1)}), bf16[4,144,72]{2,1,0:T(8,128)(2,1)S(1)}, u32[]{:S(2)}, u32[]{:S(2)}) async-start(bf16[4,144,72]{2,1,0:T(8,128)(2,1)} %copy.94), calls=%async_computation.12 | async-start | bytes 294912 | tf_op jit(solution)/shard_map/all_to_all | solution.py:144
  270.3 12.3 %all-to-all-start.7 = ((bf16[4,144,512]{2,1,0:T(8,128)(2,1)}), bf16[4,144,512]{2,1,0:T(8,128)(2,1)S(1)}, u32[]{:S(2)}, u32[]{:S(2)}) async-start(bf16[4,144,512]{2,1,0:T(8,128)(2,1)} %fusion.15), calls=%async_computation.7 | async-start | bytes 1179648 | tf_op jit(solution)/shard_map/all_to_all | solution.py:139
  282.6 11.9 %all-to-all-start.9 = ((bf16[4,144,512]{2,1,0:T(8,128)(2,1)}), bf16[4,144,512]{2,1,0:T(8,128)(2,1)S(1)}, u32[]{:S(2)}, u32[]{:S(2)}) async-start(bf16[4,144,512]{2,1,0:T(8,128)(2,1)} %fusion.14), calls=%async_computation.9 | async-start | bytes 1179648 | tf_op jit(solution)/shard_map/all_to_all | solution.py:139
  294.5 9.4 %all-to-all-start.8 = ((bf16[4,144,128]{2,1,0:T(8,128)(2,1)}), bf16[4,144,128]{2,1,0:T(8,128)(2,1)S(1)}, u32[]{:S(2)}, u32[]{:S(2)}) async-start(bf16[4,144,128]{2,1,0:T(8,128)(2,1)} %copy.88), calls=%async_computation.8 | async-start | bytes 294912 | tf_op jit(solution)/shard_map/all_to_all | solution.py:144
  303.9 9.4 %all-to-all-start.10 = ((bf16[4,144,128]{2,1,0:T(8,128)(2,1)}), bf16[4,144,128]{2,1,0:T(8,128)(2,1)S(1)}, u32[]{:S(2)}, u32[]{:S(2)}) async-start(bf16[4,144,128]{2,1,0:T(8,128)(2,1)} %copy.91), calls=%async_computation.10 | async-start | bytes 294912 | tf_op jit(solution)/shard_map/all_to_all | solution.py:144
  (17 other events, 207.3 us)
Sparse Core Ops, SparseCore 0:
  41.9 84.7 all-gather.4
  179.3 63.5 all-gather.6
